TPU v7x, 512 devices: a whole 4x4x16 slice. The times are simulated.
512 devices in a mesh: aux: 16 (over z_hi, y, core), occ: 32 (over x, z_lo).
Axes of the slice: x: 4, y: 4, z: 16 (z_hi: 2, z_lo: 8; z = z_hi * 8 + z_lo), core: 2. Of those that a mesh axis runs over, the one named last changes fastest.
Arguments:
- half_ints: bfloat16 [1024, 512, 1024], P('aux', 'occ'), may hold values from -0.71875 to 0.71875
- orbitals: bfloat16 [1024, 512], replicated, may hold values from -0.1875 to 0.1875
- eps_occ: float32 [512], replicated, may hold values from -1.5 to -0.3
- eps_vir: float32 [512], replicated, may hold values from 0.3 to 2.5
Outputs:
- density: bfloat16 [1024, 512, 512], P('aux', 'occ')
All inputs are finite; a program needn't handle non-finite values.
Results may differ from a plain program's by a relative error of at most 0.0054.
Values may be sent and summed in bfloat16 or wider, within the bound.
No kernel may reach another device: no remote copies, remote signals or barrier semaphores. Data moves between devices by JAX's collectives and lax.ppermute only.
A program may use at most 64 MiB of HBM per device.

v0:
```python
import functools

import jax
import jax.numpy as jnp
import numpy as np
from jax import lax
from jax.experimental import pallas as pl
from jax.experimental.pallas import tpu as pltpu
from jax.sharding import Mesh, PartitionSpec as P

AXES = ("zh", "y", "c", "x", "zl")
SIZES = (2, 4, 2, 4, 8)
NEAR = (3, 3)


def rank(zh, y, c, x, zl):
    return (((zh * 4 + y) * 2 + c) * 4 + x) * 8 + zl


def pairs_of(move, near):
    pairs = []
    for spot in np.ndindex(*SIZES):
        zh, y, c, x, zl = spot
        z, c2, x2 = move(zh * 8 + zl, c, x, near)
        z, x2 = z % 16, x2 % 4
        pairs.append((rank(*spot), rank(z // 8, y, c2, x2, z % 8)))
    return pairs


def outward(z, c, x, near):
    if c == z // 8 ^ x & 1:
        return z + near, 0, x
    return z + near - 6, 1, x + (1 if z % 8 >= 6 else 0)


def relay(z, c, x, near):
    if c == 0:
        return z + 1, c, x + (1 if (z - near) % 8 == 7 else 0)
    return z - 1, c, x - (1 if (z - near) % 8 == 0 else 0)


def homeward(z, c, x, near):
    owned = (z - near) % 16 // 8 ^ x & 1
    return (z - near if c == 0 else z + 8 - near), owned, x


def across(z, c, x, near):
    return z, 1 - c, x


def send(value, move, wave):
    return lax.ppermute(value, AXES, pairs_of(move, NEAR[wave]))


def exchange(value):
    return lax.all_to_all(value, ("y", "c"), split_axis=0, concat_axis=0, tiled=True)


def after(value, other):
    return lax.optimization_barrier((value, other))[0]


def cross(left, right):
    return lax.dot_general(left, right, (((0,), (0,)), ((), ())), preferred_element_type=jnp.float32)


def spread(right, amps):
    return lax.dot_general(right, amps, (((1,), (1,)), ((), ())), preferred_element_type=jnp.float32)


def pair_kernel(wave, eps, across_vir, m0, m1, m2, g0, g1, g2, out, held, met):
    zh, y, c, x, zl = (lax.axis_index(name) for name in AXES)
    spot = (zh * 8 + zl + 16 - NEAR[wave]) & 15
    own_zl = spot & 7
    own_group = x * 8 + own_zl
    row = wave * 8 + y * 2 + ((spot // 8) ^ (x & 1))
    mine, got = (m0, m1, m2), (g0, g1, g2)
    for distance in range(3):
        first = mine[distance], mine[2 - distance]
        second = got[2 - distance], got[distance]
        for core in range(2):
            for turned in range(2 if distance else 1):
                here = c == core
                if distance:
                    here = jnp.logical_and(here, (own_zl < distance) == (turned == 1))

                @pl.when(here)
                def _(a=first[core], b=second[core], turned=turned, distance=distance):
                    held[distance] = (b if turned else a)[...]
                    met[distance] = (a if turned else b)[...]

    own = eps[own_group * 16 + row]
    down_vir = jnp.transpose(jnp.broadcast_to(across_vir[...], (128, out.shape[1])))[:, :1]
    total = None
    for distance in range(3):
        gap = own + eps[((own_group + 32 - distance) & 31) * 16 + row]
        top = cross(held[0], held[distance]) + cross(met[0], met[distance])
        if distance:
            turn = cross(held[distance], held[0]) + cross(met[distance], met[0])
            top = 2.0 * top - turn
        amps = (top / (gap - down_vir - across_vir[...])).astype(jnp.bfloat16)
        part = spread(held[distance], amps)
        total = part if total is None else total + part
    out[...] = total.astype(jnp.bfloat16)


def density(wave, eps_occ, across_vir, mine, got):
    rows, nvir = mine[0].shape
    vmem = pl.BlockSpec(memory_space=pltpu.VMEM)
    return pl.pallas_call(
        functools.partial(pair_kernel, wave),
        out_shape=jax.ShapeDtypeStruct((rows, nvir), jnp.bfloat16),
        in_specs=[pl.BlockSpec(memory_space=pltpu.SMEM)] + [vmem] * 7,
        out_specs=vmem,
        scratch_shapes=[pltpu.VMEM((3, rows, nvir), jnp.bfloat16)] * 2,
        cost_estimate=pl.CostEstimate(
            flops=26 * rows * nvir * nvir, bytes_accessed=14 * rows * nvir, transcendentals=0
        ),
        compiler_params=pltpu.CompilerParams(vmem_limit_bytes=20 * 2**20),
        name="pair_stage",
    )(eps_occ, across_vir, *mine, *got)


def body(half_ints, orbitals, eps_occ, eps_vir):
    naux, _, _ = half_ints.shape
    nvir = orbitals.shape[1]
    local = lax.dot_general(
        half_ints, orbitals, (((2,), (0,)), ((), ())), preferred_element_type=jnp.float32
    ).astype(jnp.bfloat16)
    local = jnp.transpose(local, (1, 0, 2))
    across_vir = eps_vir.reshape(1, nvir)

    mine, got = ([], []), ([], [])
    pieces = [exchange(local[wave * 8 : wave * 8 + 8]).reshape(8 * naux, nvir) for wave in range(2)]
    for wave in range(2):
        mine[wave].append(send(pieces[wave], outward, wave))
    mine[0][0] = after(mine[0][0], pieces[1])
    for stage in range(2):
        got[0].append(send(mine[0][stage], across, 0))
        mine[0].append(send(mine[0][stage], relay, 0))
        mine[1][stage] = after(mine[1][stage], [got[0][stage], *got[1]])
        mine[1].append(send(mine[1][stage], relay, 1))
        if stage == 0:
            got[1].append(send(mine[1][0], across, 1))
    got[0].append(send(mine[0][2], across, 0))
    done = density(0, eps_occ, across_vir, mine[0], got[0])
    back = [send(done, homeward, 0)]
    for stage in (1, 2):
        mine[1][stage] = after(mine[1][stage], done)
        got[1].append(send(mine[1][stage], across, 1))
    done = density(1, eps_occ, across_vir, mine[1], got[1])
    back.append(send(done, homeward, 1))
    out = [exchange(value.reshape(8, naux, nvir)) for value in back]
    return jnp.concatenate([jnp.transpose(value, (1, 0, 2)) for value in out], axis=1)


def solution(mesh):
    fine = Mesh(mesh.devices.reshape(SIZES), AXES)
    placed = P(("zh", "y", "c"), ("x", "zl"), None)

    return jax.shard_map(
        body, mesh=fine, in_specs=(placed, P(), P(), P()), out_specs=placed, check_vma=False
    )
```

profile of v0, /device:TPU:2, one launch (start us, length us, event | category | flops | bytes accessed | tf_op | source)
XLA Modules:
  0.0 192.8 jit_solution(3264639505381702465)
XLA Ops:
  0.0 0.0 copy-start
  0.0 1.6 copy-done
  1.6 2.5 %fusion = bf16[16,64,512]{2,0,1:T(8,128)(2,1)S(1)} fusion(bf16[64,16,1024]{2,1,0:T(8,128)(2,1)S(1)} %copy-done, bf16[1024,512]{1,0:T(8,128)(2,1)} %param.5), kind=kOutput, calls=%fused_computation.1 | convolution fusion | flops 1074266112 | bytes 4194304 | tf_op jit(solution)/shard_map/dot_general | solution.py:127
  4.1 0.1 fusion.2
  4.1 0.0 copy-start.1
  4.2 0.0 copy-start.2
  4.2 0.2 copy.9
  4.3 14.6 %all_to_all.20 = bf16[8,64,512]{2,1,0:T(8,128)(2,1)S(1)} all-to-all(bf16[8,64,512]{2,1,0:T(8,128)(2,1)S(1)} %copy.9), channel_id=1, replica_groups=mesh['zh'=2,'y'=4,'c'=2,'x'=4,'zl'=8] {'y','c'}, dimensions={0} | all-to-all | bytes 1048576 | tf_op jit(solution)/shard_map/all_to_all | solution.py:56
  19.0 11.4 %collective-permute-start = (bf16[512,512]{1,0:T(8,128)(2,1)S(1)}, bf16[512,512]{1,0:T(8,128)(2,1)S(1)}, u32[]{:S(2)}, u32[]{:S(2)}) collective-permute-start(bf16[512,512]{1,0:T(8,128)(2,1)S(1)} %bitcast.20), channel_id=1, source_target_pairs={{0,3},{1,4},{2,5},{3,6},{4,7},{5,256},{6,257},{7,258},{8,301},{9,3... | collective-permute-start | bytes 1572872 | tf_op jit(solution)/shard_map/ppermute | solution.py:52
  30.3 0.2 copy.10
  30.5 12.8 %all_to_all.21 = bf16[8,64,512]{2,1,0:T(8,128)(2,1)S(1)} all-to-all(bf16[8,64,512]{2,1,0:T(8,128)(2,1)S(1)} %copy.10), channel_id=1, replica_groups=mesh['zh'=2,'y'=4,'c'=2,'x'=4,'zl'=8] {'y','c'}, dimensions={0} | all-to-all | bytes 1048576 | tf_op jit(solution)/shard_map/all_to_all | solution.py:56
  43.3 5.0 %collective-permute-done.m0 = bf16[512,512]{1,0:T(8,128)(2,1)S(1)} collective-permute-done((bf16[512,512]{1,0:T(8,128)(2,1)S(1)}, bf16[512,512]{1,0:T(8,128)(2,1)S(1)}, u32[]{:S(2)}, u32[]{:S(2)}) %collective-permute-start) | collective-permute-done | bytes 524320 | tf_op jit(solution)/shard_map/ppermute | solution.py:52
  48.2 3.7 %collective-permute-start.1 = (bf16[512,512]{1,0:T(8,128)(2,1)S(1)}, bf16[512,512]{1,0:T(8,128)(2,1)S(1)}, u32[]{:S(2)}, u32[]{:S(2)}) collective-permute-start(bf16[512,512]{1,0:T(8,128)(2,1)S(1)} %collective-permute-done.m0), channel_id=1, source_target_pairs={{0,1},{1,2},{2,11},{3,4},{4,5},{5,6},{6,7},{7,256},{8,9},{9,10},{1... | collective-permute-start | bytes 1572872 | tf_op jit(solution)/shard_map/ppermute | solution.py:52
  51.9 5.1 %collective-permute-start.7 = (bf16[512,512]{1,0:T(8,128)(2,1)S(1)}, bf16[512,512]{1,0:T(8,128)(2,1)S(1)}, u32[]{:S(2)}, u32[]{:S(2)}) collective-permute-start(bf16[512,512]{1,0:T(8,128)(2,1)S(1)} %bitcast.17), channel_id=1, source_target_pairs={{0,3},{1,4},{2,5},{3,6},{4,7},{5,256},{6,257},{7,258},{8,301},{9,3... | collective-permute-start | bytes 1572872 | tf_op jit(solution)/shard_map/ppermute | solution.py:52
  57.0 1.9 collective-permute-start.3
  58.9 7.4 %collective-permute-done.1.m1 = bf16[512,512]{1,0:T(8,128)(2,1)S(1)} collective-permute-done((bf16[512,512]{1,0:T(8,128)(2,1)S(1)}, bf16[512,512]{1,0:T(8,128)(2,1)S(1)}, u32[]{:S(2)}, u32[]{:S(2)}) %collective-permute-start.1) | collective-permute-done | bytes 524320 | tf_op jit(solution)/shard_map/ppermute | solution.py:52
  66.3 12.1 %collective-permute-start.2 = (bf16[512,512]{1,0:T(8,128)(2,1)S(1)}, bf16[512,512]{1,0:T(8,128)(2,1)S(1)}, u32[]{:S(2)}, u32[]{:S(2)}) collective-permute-start(bf16[512,512]{1,0:T(8,128)(2,1)S(1)} %collective-permute-done.1.m1), channel_id=1, source_target_pairs={{0,1},{1,2},{2,11},{3,4},{4,5},{5,6},{6,7},{7,256},{8,9},{9,10},{1... | collective-permute-start | bytes 1572872 | tf_op jit(solution)/shard_map/ppermute | solution.py:52
  78.4 0.0 collective-permute-done.7.m0
  78.4 0.0 collective-permute-done.3.g0
  78.4 1.9 collective-permute-start.4
  80.3 2.4 %collective-permute-start.9 = (bf16[512,512]{1,0:T(8,128)(2,1)S(1)}, bf16[512,512]{1,0:T(8,128)(2,1)S(1)}, u32[]{:S(2)}, u32[]{:S(2)}) collective-permute-start(bf16[512,512]{1,0:T(8,128)(2,1)S(1)} %collective-permute-done.7.m0), channel_id=1, source_target_pairs={{0,32},{1,33},{2,34},{3,35},{4,36},{5,37},{6,38},{7,39},{8,40},{9,... | collective-permute-start | bytes 1572872 | tf_op jit(solution)/shard_map/ppermute | solution.py:52
  82.7 5.2 %collective-permute-start.8 = (bf16[512,512]{1,0:T(8,128)(2,1)S(1)}, bf16[512,512]{1,0:T(8,128)(2,1)S(1)}, u32[]{:S(2)}, u32[]{:S(2)}) collective-permute-start(bf16[512,512]{1,0:T(8,128)(2,1)S(1)} %collective-permute-done.7.m0), channel_id=1, source_target_pairs={{0,1},{1,2},{2,11},{3,4},{4,5},{5,6},{6,7},{7,256},{8,9},{9,10},{1... | collective-permute-start | bytes 1572872 | tf_op jit(solution)/shard_map/ppermute | solution.py:52
  87.9 0.0 collective-permute-done.2.m2
  87.9 1.9 collective-permute-start.5
  89.9 0.0 collective-permute-done.4.g1
  89.9 0.0 collective-permute-done.9.g0
  89.9 5.1 %collective-permute-done.8.m1 = bf16[512,512]{1,0:T(8,128)(2,1)S(1)} collective-permute-done((bf16[512,512]{1,0:T(8,128)(2,1)S(1)}, bf16[512,512]{1,0:T(8,128)(2,1)S(1)}, u32[]{:S(2)}, u32[]{:S(2)}) %collective-permute-start.8) | collective-permute-done | bytes 524320 | tf_op jit(solution)/shard_map/ppermute | solution.py:52
  95.0 4.0 %collective-permute-start.10 = (bf16[512,512]{1,0:T(8,128)(2,1)S(1)}, bf16[512,512]{1,0:T(8,128)(2,1)S(1)}, u32[]{:S(2)}, u32[]{:S(2)}) collective-permute-start(bf16[512,512]{1,0:T(8,128)(2,1)S(1)} %collective-permute-done.8.m1), channel_id=1, source_target_pairs={{0,1},{1,2},{2,11},{3,4},{4,5},{5,6},{6,7},{7,256},{8,9},{9,10},{1... | collective-permute-start | bytes 1572872 | tf_op jit(solution)/shard_map/ppermute | solution.py:52
  99.0 0.0 collective-permute-done.5.g2
  99.0 0.0 copy-done.1
  99.0 0.0 copy-done.2
  99.0 4.7 %pair_stage.2 = bf16[512,512]{1,0:T(8,128)(2,1)S(1)} custom-call(f32[512]{0:T(512)S(1)} %copy-done.1, f32[1,512]{1,0:T(1,128)S(1)} %bitcast.13, bf16[512,512]{1,0:T(8,128)(2,1)S(1)} %collective-permute-done.m0, bf16[512,512]{1,0:T(8,128)(2,1)S(1)} %collective-permute-done.1.m1, bf16[512,512]{1,0:T(8,128)(2,1)S(1)} %collective-permute-done.2.m2, ...), custom_call_target="tpu_custom_call" | custom-call | flops 3489660928 | bytes 3670016 | tf_op jit(solution)/shard_map/pair_stage/pallas_call | solution.py:110
  103.8 3.5 %collective-permute-done.10.m2 = bf16[512,512]{1,0:T(8,128)(2,1)S(1)} collective-permute-done((bf16[512,512]{1,0:T(8,128)(2,1)S(1)}, bf16[512,512]{1,0:T(8,128)(2,1)S(1)}, u32[]{:S(2)}, u32[]{:S(2)}) %collective-permute-start.10) | collective-permute-done | bytes 524320 | tf_op jit(solution)/shard_map/ppermute | solution.py:52
  107.3 1.9 collective-permute-start.12
  109.2 2.4 %collective-permute-start.11 = (bf16[512,512]{1,0:T(8,128)(2,1)S(1)}, bf16[512,512]{1,0:T(8,128)(2,1)S(1)}, u32[]{:S(2)}, u32[]{:S(2)}) collective-permute-start(bf16[512,512]{1,0:T(8,128)(2,1)S(1)} %collective-permute-done.8.m1), channel_id=1, source_target_pairs={{0,32},{1,33},{2,34},{3,35},{4,36},{5,37},{6,38},{7,39},{8,40},{9,... | collective-permute-start | bytes 1572872 | tf_op jit(solution)/shard_map/ppermute | solution.py:52
  111.6 5.7 %collective-permute-start.6 = (bf16[512,512]{1,0:T(8,128)(2,1)S(1)}, bf16[512,512]{1,0:T(8,128)(2,1)S(1)}, u32[]{:S(2)}, u32[]{:S(2)}) collective-permute-start(bf16[512,512]{1,0:T(8,128)(2,1)S(1)} %pair_stage.2), channel_id=1, source_target_pairs={{0,293},{1,294},{2,295},{3,0},{4,1},{5,2},{6,3},{7,4},{8,269},{9,2... | collective-permute-start | bytes 1572872 | tf_op jit(solution)/shard_map/ppermute | solution.py:52
  117.3 0.0 collective-permute-done.12.g2
  117.3 0.0 collective-permute-done.11.g1
  117.3 4.7 %pair_stage.3 = bf16[512,512]{1,0:T(8,128)(2,1)S(1)} custom-call(f32[512]{0:T(512)S(1)} %copy-done.1, f32[1,512]{1,0:T(1,128)S(1)} %bitcast.14, bf16[512,512]{1,0:T(8,128)(2,1)S(1)} %collective-permute-done.7.m0, bf16[512,512]{1,0:T(8,128)(2,1)S(1)} %collective-permute-done.8.m1, bf16[512,512]{1,0:T(8,128)(2,1)S(1)} %collective-permute-done.10.m2, ...), custom_call_target="tpu_custom_call" | custom-call | flops 3489660928 | bytes 3670016 | tf_op jit(solution)/shard_map/pair_stage/pallas_call | solution.py:110
  122.1 4.2 %collective-permute-start.13 = (bf16[512,512]{1,0:T(8,128)(2,1)S(1)}, bf16[512,512]{1,0:T(8,128)(2,1)S(1)}, u32[]{:S(2)}, u32[]{:S(2)}) collective-permute-start(bf16[512,512]{1,0:T(8,128)(2,1)S(1)} %pair_stage.3), channel_id=1, source_target_pairs={{0,293},{1,294},{2,295},{3,0},{4,1},{5,2},{6,3},{7,4},{8,269},{9,2... | collective-permute-start | bytes 1572872 | tf_op jit(solution)/shard_map/ppermute | solution.py:52
  126.3 22.1 %collective-permute-done.6 = bf16[512,512]{1,0:T(8,128)(2,1)S(1)} collective-permute-done((bf16[512,512]{1,0:T(8,128)(2,1)S(1)}, bf16[512,512]{1,0:T(8,128)(2,1)S(1)}, u32[]{:S(2)}, u32[]{:S(2)}) %collective-permute-start.6) | collective-permute-done | bytes 524320 | tf_op jit(solution)/shard_map/ppermute | solution.py:52
  148.4 12.8 %all_to_all.22 = bf16[8,64,512]{2,1,0:T(8,128)(2,1)S(1)} all-to-all(bf16[8,64,512]{2,1,0:T(8,128)(2,1)S(1)} %bitcast.18), channel_id=1, replica_groups=mesh['zh'=2,'y'=4,'c'=2,'x'=4,'zl'=8] {'y','c'}, dimensions={0} | all-to-all | bytes 1048576 | tf_op jit(solution)/shard_map/all_to_all | solution.py:56
  161.1 17.3 %collective-permute-done.13 = bf16[512,512]{1,0:T(8,128)(2,1)S(1)} collective-permute-done((bf16[512,512]{1,0:T(8,128)(2,1)S(1)}, bf16[512,512]{1,0:T(8,128)(2,1)S(1)}, u32[]{:S(2)}, u32[]{:S(2)}) %collective-permute-start.13) | collective-permute-done | bytes 524320 | tf_op jit(solution)/shard_map/ppermute | solution.py:52
  178.4 12.8 %all_to_all.23 = bf16[8,64,512]{2,1,0:T(8,128)(2,1)S(1)} all-to-all(bf16[8,64,512]{2,1,0:T(8,128)(2,1)S(1)} %bitcast.19), channel_id=1, replica_groups=mesh['zh'=2,'y'=4,'c'=2,'x'=4,'zl'=8] {'y','c'}, dimensions={0} | all-to-all | bytes 1048576 | tf_op jit(solution)/shard_map/all_to_all | solution.py:56
  191.2 0.1 pad_maximum_fusion
  191.3 1.5 copy.11
Async XLA Ops:
  0.0 1.6 copy-start
  4.1 94.9 %copy-start.1 = (f32[512]{0:T(512)S(1)}, f32[512]{0:T(512)}, u32[]{:S(2)}) copy-start(f32[512]{0:T(512)} %eps.3) | copy-start | bytes 6148
  4.2 94.9 %copy-start.2 = (f32[512]{0:T(512)S(1)}, f32[512]{0:T(512)}, u32[]{:S(2)}) copy-start(f32[512]{0:T(512)} %param.7) | copy-start | bytes 6148
  19.0 29.3 %collective-permute-start = (bf16[512,512]{1,0:T(8,128)(2,1)S(1)}, bf16[512,512]{1,0:T(8,128)(2,1)S(1)}, u32[]{:S(2)}, u32[]{:S(2)}) collective-permute-start(bf16[512,512]{1,0:T(8,128)(2,1)S(1)} %bitcast.20), channel_id=1, source_target_pairs={{0,3},{1,4},{2,5},{3,6},{4,7},{5,256},{6,257},{7,258},{8,301},{9,3... | collective-permute-start | bytes 1572872 | tf_op jit(solution)/shard_map/ppermute | solution.py:52
  48.2 18.0 %collective-permute-start.1 = (bf16[512,512]{1,0:T(8,128)(2,1)S(1)}, bf16[512,512]{1,0:T(8,128)(2,1)S(1)}, u32[]{:S(2)}, u32[]{:S(2)}) collective-permute-start(bf16[512,512]{1,0:T(8,128)(2,1)S(1)} %collective-permute-done.m0), channel_id=1, source_target_pairs={{0,1},{1,2},{2,11},{3,4},{4,5},{5,6},{6,7},{7,256},{8,9},{9,10},{1... | collective-permute-start | bytes 1572872 | tf_op jit(solution)/shard_map/ppermute | solution.py:52
  51.9 26.5 %collective-permute-start.7 = (bf16[512,512]{1,0:T(8,128)(2,1)S(1)}, bf16[512,512]{1,0:T(8,128)(2,1)S(1)}, u32[]{:S(2)}, u32[]{:S(2)}) collective-permute-start(bf16[512,512]{1,0:T(8,128)(2,1)S(1)} %bitcast.17), channel_id=1, source_target_pairs={{0,3},{1,4},{2,5},{3,6},{4,7},{5,256},{6,257},{7,258},{8,301},{9,3... | collective-permute-start | bytes 1572872 | tf_op jit(solution)/shard_map/ppermute | solution.py:52
  57.0 21.4 %collective-permute-start.3 = (bf16[512,512]{1,0:T(8,128)(2,1)S(1)}, bf16[512,512]{1,0:T(8,128)(2,1)S(1)}, u32[]{:S(2)}, u32[]{:S(2)}) collective-permute-start(bf16[512,512]{1,0:T(8,128)(2,1)S(1)} %collective-permute-done.m0), channel_id=1, source_target_pairs={{0,32},{1,33},{2,34},{3,35},{4,36},{5,37},{6,38},{7,39},{8,40},{9,... | collective-permute-start | bytes 1572872 | tf_op jit(solution)/shard_map/ppermute | solution.py:52
  66.3 21.7 %collective-permute-start.2 = (bf16[512,512]{1,0:T(8,128)(2,1)S(1)}, bf16[512,512]{1,0:T(8,128)(2,1)S(1)}, u32[]{:S(2)}, u32[]{:S(2)}) collective-permute-start(bf16[512,512]{1,0:T(8,128)(2,1)S(1)} %collective-permute-done.1.m1), channel_id=1, source_target_pairs={{0,1},{1,2},{2,11},{3,4},{4,5},{5,6},{6,7},{7,256},{8,9},{9,10},{1... | collective-permute-start | bytes 1572872 | tf_op jit(solution)/shard_map/ppermute | solution.py:52
  78.4 11.5 %collective-permute-start.4 = (bf16[512,512]{1,0:T(8,128)(2,1)S(1)}, bf16[512,512]{1,0:T(8,128)(2,1)S(1)}, u32[]{:S(2)}, u32[]{:S(2)}) collective-permute-start(bf16[512,512]{1,0:T(8,128)(2,1)S(1)} %collective-permute-done.1.m1), channel_id=1, source_target_pairs={{0,32},{1,33},{2,34},{3,35},{4,36},{5,37},{6,38},{7,39},{8,40},{9,... | collective-permute-start | bytes 1572872 | tf_op jit(solution)/shard_map/ppermute | solution.py:52
  80.3 9.6 %collective-permute-start.9 = (bf16[512,512]{1,0:T(8,128)(2,1)S(1)}, bf16[512,512]{1,0:T(8,128)(2,1)S(1)}, u32[]{:S(2)}, u32[]{:S(2)}) collective-permute-start(bf16[512,512]{1,0:T(8,128)(2,1)S(1)} %collective-permute-done.7.m0), channel_id=1, source_target_pairs={{0,32},{1,33},{2,34},{3,35},{4,36},{5,37},{6,38},{7,39},{8,40},{9,... | collective-permute-start | bytes 1572872 | tf_op jit(solution)/shard_map/ppermute | solution.py:52
  82.7 12.3 %collective-permute-start.8 = (bf16[512,512]{1,0:T(8,128)(2,1)S(1)}, bf16[512,512]{1,0:T(8,128)(2,1)S(1)}, u32[]{:S(2)}, u32[]{:S(2)}) collective-permute-start(bf16[512,512]{1,0:T(8,128)(2,1)S(1)} %collective-permute-done.7.m0), channel_id=1, source_target_pairs={{0,1},{1,2},{2,11},{3,4},{4,5},{5,6},{6,7},{7,256},{8,9},{9,10},{1... | collective-permute-start | bytes 1572872 | tf_op jit(solution)/shard_map/ppermute | solution.py:52
  87.9 11.1 %collective-permute-start.5 = (bf16[512,512]{1,0:T(8,128)(2,1)S(1)}, bf16[512,512]{1,0:T(8,128)(2,1)S(1)}, u32[]{:S(2)}, u32[]{:S(2)}) collective-permute-start(bf16[512,512]{1,0:T(8,128)(2,1)S(1)} %collective-permute-done.2.m2), channel_id=1, source_target_pairs={{0,32},{1,33},{2,34},{3,35},{4,36},{5,37},{6,38},{7,39},{8,40},{9,... | collective-permute-start | bytes 1572872 | tf_op jit(solution)/shard_map/ppermute | solution.py:52
  95.0 12.3 %collective-permute-start.10 = (bf16[512,512]{1,0:T(8,128)(2,1)S(1)}, bf16[512,512]{1,0:T(8,128)(2,1)S(1)}, u32[]{:S(2)}, u32[]{:S(2)}) collective-permute-start(bf16[512,512]{1,0:T(8,128)(2,1)S(1)} %collective-permute-done.8.m1), channel_id=1, source_target_pairs={{0,1},{1,2},{2,11},{3,4},{4,5},{5,6},{6,7},{7,256},{8,9},{9,10},{1... | collective-permute-start | bytes 1572872 | tf_op jit(solution)/shard_map/ppermute | solution.py:52
  107.3 10.0 %collective-permute-start.12 = (bf16[512,512]{1,0:T(8,128)(2,1)S(1)}, bf16[512,512]{1,0:T(8,128)(2,1)S(1)}, u32[]{:S(2)}, u32[]{:S(2)}) collective-permute-start(bf16[512,512]{1,0:T(8,128)(2,1)S(1)} %collective-permute-done.10.m2), channel_id=1, source_target_pairs={{0,32},{1,33},{2,34},{3,35},{4,36},{5,37},{6,38},{7,39},{8,40},{9,... | collective-permute-start | bytes 1572872 | tf_op jit(solution)/shard_map/ppermute | solution.py:52
  109.2 8.1 %collective-permute-start.11 = (bf16[512,512]{1,0:T(8,128)(2,1)S(1)}, bf16[512,512]{1,0:T(8,128)(2,1)S(1)}, u32[]{:S(2)}, u32[]{:S(2)}) collective-permute-start(bf16[512,512]{1,0:T(8,128)(2,1)S(1)} %collective-permute-done.8.m1), channel_id=1, source_target_pairs={{0,32},{1,33},{2,34},{3,35},{4,36},{5,37},{6,38},{7,39},{8,40},{9,... | collective-permute-start | bytes 1572872 | tf_op jit(solution)/shard_map/ppermute | solution.py:52
  111.6 36.7 %collective-permute-start.6 = (bf16[512,512]{1,0:T(8,128)(2,1)S(1)}, bf16[512,512]{1,0:T(8,128)(2,1)S(1)}, u32[]{:S(2)}, u32[]{:S(2)}) collective-permute-start(bf16[512,512]{1,0:T(8,128)(2,1)S(1)} %pair_stage.2), channel_id=1, source_target_pairs={{0,293},{1,294},{2,295},{3,0},{4,1},{5,2},{6,3},{7,4},{8,269},{9,2... | collective-permute-start | bytes 1572872 | tf_op jit(solution)/shard_map/ppermute | solution.py:52
  122.1 56.4 %collective-permute-start.13 = (bf16[512,512]{1,0:T(8,128)(2,1)S(1)}, bf16[512,512]{1,0:T(8,128)(2,1)S(1)}, u32[]{:S(2)}, u32[]{:S(2)}) collective-permute-start(bf16[512,512]{1,0:T(8,128)(2,1)S(1)} %pair_stage.3), channel_id=1, source_target_pairs={{0,293},{1,294},{2,295},{3,0},{4,1},{5,2},{6,3},{7,4},{8,269},{9,2... | collective-permute-start | bytes 1572872 | tf_op jit(solution)/shard_map/ppermute | solution.py:52
where the time goes:
time: 194 us; the launch traced here: 193 us
  starting transfers between devices  63.7 us (33%)
  waiting for transfers between devices  60.4 us (31%)
  blocking collectives  52.9 us (27%)
  Pallas kernels  9.46 us (5%)
  local copies, waits for them, and re-layouts  3.54 us (2%)
  matrix products  2.46 us (1%)
    ppermute x14, starting transfers between devices, send(): return lax.ppermute(value, AXES, pairs_of(move, NEAR[wave]))  63.7 us
    ppermute x14, waiting for transfers between devices, send(): return lax.ppermute(value, AXES, pairs_of(move, NEAR[wave]))  60.4 us
    all_to_all x4, blocking collectives, exchange(): lax.all_to_all(value, ('y', 'c'), split_axis=0, concat_axis=0, tiled=True)  52.9 us
    pallas_call x2, Pallas kernels, density(): pl.pallas_call(functools.partial(pair_kernel, wave), out_shape=jax.ShapeD...  9.46 us
  transfers between devices with their start and end apart: 14, of which 6 were waited for; matrix products, arithmetic and copies ran while one was open for 0% of the time, Pallas kernels for 5%

commit v1 on v0

--- a/solution.py
+++ b/solution.py
@@ -138,16 +138,18 @@
     for stage in range(2):
         got[0].append(send(mine[0][stage], across, 0))
         mine[0].append(send(mine[0][stage], relay, 0))
-        mine[1][stage] = after(mine[1][stage], [got[0][stage], *got[1]])
-        mine[1].append(send(mine[1][stage], relay, 1))
         if stage == 0:
+            mine[1][0] = after(mine[1][0], got[0][0])
+            mine[1].append(send(mine[1][0], relay, 1))
             got[1].append(send(mine[1][0], across, 1))
     got[0].append(send(mine[0][2], across, 0))
     done = density(0, eps_occ, across_vir, mine[0], got[0])
     back = [send(done, homeward, 0)]
-    for stage in (1, 2):
-        mine[1][stage] = after(mine[1][stage], done)
-        got[1].append(send(mine[1][stage], across, 1))
+    mine[1][1] = after(mine[1][1], [done, got[1][0]])
+    mine[1].append(send(mine[1][1], relay, 1))
+    got[1].append(send(mine[1][1], across, 1))
+    mine[1][2] = after(mine[1][2], got[1][1])
+    got[1].append(send(mine[1][2], across, 1))
     done = density(1, eps_occ, across_vir, mine[1], got[1])
     back.append(send(done, homeward, 1))
     out = [exchange(value.reshape(8, naux, nvir)) for value in back]

time: 194 us -> 203 us (1.046)
  waiting for transfers between devices: 60.4 us -> 79.3 us
  starting transfers between devices: 63.7 us -> 54.5 us
    ppermute x14, waiting for transfers between devices: 60.4 us -> 79.3 us  [send(): return lax.ppermute(value, AXES, pairs_of(move, NEAR[wave]))]
    ppermute x14, starting transfers between devices: 63.7 us -> 54.5 us  [send(): return lax.ppermute(value, AXES, pairs_of(move, NEAR[wave]))]
  transfers between devices with their start and end apart: 14 -> 14, of which waited for: 6 -> 8; matrix products, arithmetic and copies ran while one was open for 0% -> 0% of each run, Pallas kernels for 5% -> 5%
where the time goes in v1:
time: 203 us; the launch traced here: 202 us
  waiting for transfers between devices  79.3 us (39%)
  starting transfers between devices  54.5 us (27%)
  blocking collectives  52.9 us (26%)
  Pallas kernels  9.46 us (5%)
  local copies, waits for them, and re-layouts  3.54 us (2%)
  matrix products  2.46 us (1%)
    ppermute x14, waiting for transfers between devices, send(): return lax.ppermute(value, AXES, pairs_of(move, NEAR[wave]))  79.3 us
    ppermute x14, starting transfers between devices, send(): return lax.ppermute(value, AXES, pairs_of(move, NEAR[wave]))  54.5 us
    all_to_all x4, blocking collectives, exchange(): lax.all_to_all(value, ('y', 'c'), split_axis=0, concat_axis=0, tiled=True)  52.9 us
    pallas_call x2, Pallas kernels, density(): pl.pallas_call(functools.partial(pair_kernel, wave), out_shape=jax.ShapeD...  9.46 us
  transfers between devices with their start and end apart: 14, of which 8 were waited for; matrix products, arithmetic and copies ran while one was open for 0% of the time, Pallas kernels for 5%

profile of v1, /device:TPU:2, one launch (start us, length us, event | category | flops | bytes accessed | tf_op | source)
XLA Modules:
  0.0 202.5 jit_solution(14095161638228110160)
XLA Ops:
  0.0 0.0 copy-start
  0.0 1.6 copy-done
  1.6 2.5 %fusion = bf16[16,64,512]{2,0,1:T(8,128)(2,1)S(1)} fusion(bf16[64,16,1024]{2,1,0:T(8,128)(2,1)S(1)} %copy-done, bf16[1024,512]{1,0:T(8,128)(2,1)} %param.5), kind=kOutput, calls=%fused_computation.1 | convolution fusion | flops 1074266112 | bytes 4194304 | tf_op jit(solution)/shard_map/dot_general | solution.py:127
  4.1 0.1 fusion.2
  4.1 0.0 copy-start.1
  4.2 0.0 copy-start.2
  4.2 0.2 copy.9
  4.3 14.6 %all_to_all.20 = bf16[8,64,512]{2,1,0:T(8,128)(2,1)S(1)} all-to-all(bf16[8,64,512]{2,1,0:T(8,128)(2,1)S(1)} %copy.9), channel_id=1, replica_groups=mesh['zh'=2,'y'=4,'c'=2,'x'=4,'zl'=8] {'y','c'}, dimensions={0} | all-to-all | bytes 1048576 | tf_op jit(solution)/shard_map/all_to_all | solution.py:56
  19.0 11.4 %collective-permute-start = (bf16[512,512]{1,0:T(8,128)(2,1)S(1)}, bf16[512,512]{1,0:T(8,128)(2,1)S(1)}, u32[]{:S(2)}, u32[]{:S(2)}) collective-permute-start(bf16[512,512]{1,0:T(8,128)(2,1)S(1)} %bitcast.20), channel_id=1, source_target_pairs={{0,3},{1,4},{2,5},{3,6},{4,7},{5,256},{6,257},{7,258},{8,301},{9,3... | collective-permute-start | bytes 1572872 | tf_op jit(solution)/shard_map/ppermute | solution.py:52
  30.3 0.2 copy.10
  30.5 12.8 %all_to_all.21 = bf16[8,64,512]{2,1,0:T(8,128)(2,1)S(1)} all-to-all(bf16[8,64,512]{2,1,0:T(8,128)(2,1)S(1)} %copy.10), channel_id=1, replica_groups=mesh['zh'=2,'y'=4,'c'=2,'x'=4,'zl'=8] {'y','c'}, dimensions={0} | all-to-all | bytes 1048576 | tf_op jit(solution)/shard_map/all_to_all | solution.py:56
  43.3 5.0 %collective-permute-done.m0 = bf16[512,512]{1,0:T(8,128)(2,1)S(1)} collective-permute-done((bf16[512,512]{1,0:T(8,128)(2,1)S(1)}, bf16[512,512]{1,0:T(8,128)(2,1)S(1)}, u32[]{:S(2)}, u32[]{:S(2)}) %collective-permute-start) | collective-permute-done | bytes 524320 | tf_op jit(solution)/shard_map/ppermute | solution.py:52
  48.2 3.7 %collective-permute-start.1 = (bf16[512,512]{1,0:T(8,128)(2,1)S(1)}, bf16[512,512]{1,0:T(8,128)(2,1)S(1)}, u32[]{:S(2)}, u32[]{:S(2)}) collective-permute-start(bf16[512,512]{1,0:T(8,128)(2,1)S(1)} %collective-permute-done.m0), channel_id=1, source_target_pairs={{0,1},{1,2},{2,11},{3,4},{4,5},{5,6},{6,7},{7,256},{8,9},{9,10},{1... | collective-permute-start | bytes 1572872 | tf_op jit(solution)/shard_map/ppermute | solution.py:52
  51.9 9.9 %collective-permute-done.1.m1 = bf16[512,512]{1,0:T(8,128)(2,1)S(1)} collective-permute-done((bf16[512,512]{1,0:T(8,128)(2,1)S(1)}, bf16[512,512]{1,0:T(8,128)(2,1)S(1)}, u32[]{:S(2)}, u32[]{:S(2)}) %collective-permute-start.1) | collective-permute-done | bytes 524320 | tf_op jit(solution)/shard_map/ppermute | solution.py:52
  61.8 1.9 collective-permute-start.2
  63.7 3.4 %collective-permute-start.7 = (bf16[512,512]{1,0:T(8,128)(2,1)S(1)}, bf16[512,512]{1,0:T(8,128)(2,1)S(1)}, u32[]{:S(2)}, u32[]{:S(2)}) collective-permute-start(bf16[512,512]{1,0:T(8,128)(2,1)S(1)} %bitcast.17), channel_id=1, source_target_pairs={{0,3},{1,4},{2,5},{3,6},{4,7},{5,256},{6,257},{7,258},{8,301},{9,3... | collective-permute-start | bytes 1572872 | tf_op jit(solution)/shard_map/ppermute | solution.py:52
  67.2 1.9 collective-permute-start.3
  69.1 2.4 %collective-permute-start.4 = (bf16[512,512]{1,0:T(8,128)(2,1)S(1)}, bf16[512,512]{1,0:T(8,128)(2,1)S(1)}, u32[]{:S(2)}, u32[]{:S(2)}) collective-permute-start(bf16[512,512]{1,0:T(8,128)(2,1)S(1)} %collective-permute-done.1.m1), channel_id=1, source_target_pairs={{0,32},{1,33},{2,34},{3,35},{4,36},{5,37},{6,38},{7,39},{8,40},{9,... | collective-permute-start | bytes 1572872 | tf_op jit(solution)/shard_map/ppermute | solution.py:52
  71.5 5.3 %collective-permute-done.2.m2 = bf16[512,512]{1,0:T(8,128)(2,1)S(1)} collective-permute-done((bf16[512,512]{1,0:T(8,128)(2,1)S(1)}, bf16[512,512]{1,0:T(8,128)(2,1)S(1)}, u32[]{:S(2)}, u32[]{:S(2)}) %collective-permute-start.2) | collective-permute-done | bytes 524320 | tf_op jit(solution)/shard_map/ppermute | solution.py:52
  76.8 1.9 collective-permute-start.5
  78.7 6.3 %collective-permute-done.7.m0 = bf16[512,512]{1,0:T(8,128)(2,1)S(1)} collective-permute-done((bf16[512,512]{1,0:T(8,128)(2,1)S(1)}, bf16[512,512]{1,0:T(8,128)(2,1)S(1)}, u32[]{:S(2)}, u32[]{:S(2)}) %collective-permute-start.7) | collective-permute-done | bytes 524320 | tf_op jit(solution)/shard_map/ppermute | solution.py:52
  85.1 0.0 collective-permute-done.3.g0
  85.1 1.9 collective-permute-start.9
  87.0 9.5 %collective-permute-start.8 = (bf16[512,512]{1,0:T(8,128)(2,1)S(1)}, bf16[512,512]{1,0:T(8,128)(2,1)S(1)}, u32[]{:S(2)}, u32[]{:S(2)}) collective-permute-start(bf16[512,512]{1,0:T(8,128)(2,1)S(1)} %collective-permute-done.7.m0), channel_id=1, source_target_pairs={{0,1},{1,2},{2,11},{3,4},{4,5},{5,6},{6,7},{7,256},{8,9},{9,10},{1... | collective-permute-start | bytes 1572872 | tf_op jit(solution)/shard_map/ppermute | solution.py:52
  96.5 0.0 collective-permute-done.4.g1
  96.5 0.0 collective-permute-done.5.g2
  96.5 0.0 copy-done.1
  96.5 0.0 copy-done.2
  96.5 4.7 %pair_stage.2 = bf16[512,512]{1,0:T(8,128)(2,1)S(1)} custom-call(f32[512]{0:T(512)S(1)} %copy-done.1, f32[1,512]{1,0:T(1,128)S(1)} %bitcast.13, bf16[512,512]{1,0:T(8,128)(2,1)S(1)} %collective-permute-done.m0, bf16[512,512]{1,0:T(8,128)(2,1)S(1)} %collective-permute-done.1.m1, bf16[512,512]{1,0:T(8,128)(2,1)S(1)} %collective-permute-done.2.m2, ...), custom_call_target="tpu_custom_call" | custom-call | flops 3489660928 | bytes 3670016 | tf_op jit(solution)/shard_map/pair_stage/pallas_call | solution.py:110
  101.3 0.0 collective-permute-done.9.g0
  101.3 1.9 collective-permute-done.8.m1
  103.2 2.0 collective-permute-start.11
  105.2 4.3 %collective-permute-start.10 = (bf16[512,512]{1,0:T(8,128)(2,1)S(1)}, bf16[512,512]{1,0:T(8,128)(2,1)S(1)}, u32[]{:S(2)}, u32[]{:S(2)}) collective-permute-start(bf16[512,512]{1,0:T(8,128)(2,1)S(1)} %collective-permute-done.8.m1), channel_id=1, source_target_pairs={{0,1},{1,2},{2,11},{3,4},{4,5},{5,6},{6,7},{7,256},{8,9},{9,10},{1... | collective-permute-start | bytes 1572872 | tf_op jit(solution)/shard_map/ppermute | solution.py:52
  109.5 0.0 collective-permute-done.11.g1
  109.5 9.5 %collective-permute-done.10.m2 = bf16[512,512]{1,0:T(8,128)(2,1)S(1)} collective-permute-done((bf16[512,512]{1,0:T(8,128)(2,1)S(1)}, bf16[512,512]{1,0:T(8,128)(2,1)S(1)}, u32[]{:S(2)}, u32[]{:S(2)}) %collective-permute-start.10) | collective-permute-done | bytes 524320 | tf_op jit(solution)/shard_map/ppermute | solution.py:52
  119.0 1.9 collective-permute-start.12
  120.9 4.5 %collective-permute-start.6 = (bf16[512,512]{1,0:T(8,128)(2,1)S(1)}, bf16[512,512]{1,0:T(8,128)(2,1)S(1)}, u32[]{:S(2)}, u32[]{:S(2)}) collective-permute-start(bf16[512,512]{1,0:T(8,128)(2,1)S(1)} %pair_stage.2), channel_id=1, source_target_pairs={{0,293},{1,294},{2,295},{3,0},{4,1},{5,2},{6,3},{7,4},{8,269},{9,2... | collective-permute-start | bytes 1572872 | tf_op jit(solution)/shard_map/ppermute | solution.py:52
  125.4 0.0 collective-permute-done.12.g2
  125.4 4.7 %pair_stage.3 = bf16[512,512]{1,0:T(8,128)(2,1)S(1)} custom-call(f32[512]{0:T(512)S(1)} %copy-done.1, f32[1,512]{1,0:T(1,128)S(1)} %bitcast.14, bf16[512,512]{1,0:T(8,128)(2,1)S(1)} %collective-permute-done.7.m0, bf16[512,512]{1,0:T(8,128)(2,1)S(1)} %collective-permute-done.8.m1, bf16[512,512]{1,0:T(8,128)(2,1)S(1)} %collective-permute-done.10.m2, ...), custom_call_target="tpu_custom_call" | custom-call | flops 3489660928 | bytes 3670016 | tf_op jit(solution)/shard_map/pair_stage/pallas_call | solution.py:110
  130.2 3.7 %collective-permute-start.13 = (bf16[512,512]{1,0:T(8,128)(2,1)S(1)}, bf16[512,512]{1,0:T(8,128)(2,1)S(1)}, u32[]{:S(2)}, u32[]{:S(2)}) collective-permute-start(bf16[512,512]{1,0:T(8,128)(2,1)S(1)} %pair_stage.3), channel_id=1, source_target_pairs={{0,293},{1,294},{2,295},{3,0},{4,1},{5,2},{6,3},{7,4},{8,269},{9,2... | collective-permute-start | bytes 1572872 | tf_op jit(solution)/shard_map/ppermute | solution.py:52
  133.9 20.1 %collective-permute-done.6 = bf16[512,512]{1,0:T(8,128)(2,1)S(1)} collective-permute-done((bf16[512,512]{1,0:T(8,128)(2,1)S(1)}, bf16[512,512]{1,0:T(8,128)(2,1)S(1)}, u32[]{:S(2)}, u32[]{:S(2)}) %collective-permute-start.6) | collective-permute-done | bytes 524320 | tf_op jit(solution)/shard_map/ppermute | solution.py:52
  154.0 12.8 %all_to_all.22 = bf16[8,64,512]{2,1,0:T(8,128)(2,1)S(1)} all-to-all(bf16[8,64,512]{2,1,0:T(8,128)(2,1)S(1)} %bitcast.18), channel_id=1, replica_groups=mesh['zh'=2,'y'=4,'c'=2,'x'=4,'zl'=8] {'y','c'}, dimensions={0} | all-to-all | bytes 1048576 | tf_op jit(solution)/shard_map/all_to_all | solution.py:56
  166.8 21.3 %collective-permute-done.13 = bf16[512,512]{1,0:T(8,128)(2,1)S(1)} collective-permute-done((bf16[512,512]{1,0:T(8,128)(2,1)S(1)}, bf16[512,512]{1,0:T(8,128)(2,1)S(1)}, u32[]{:S(2)}, u32[]{:S(2)}) %collective-permute-start.13) | collective-permute-done | bytes 524320 | tf_op jit(solution)/shard_map/ppermute | solution.py:52
  188.1 12.8 %all_to_all.23 = bf16[8,64,512]{2,1,0:T(8,128)(2,1)S(1)} all-to-all(bf16[8,64,512]{2,1,0:T(8,128)(2,1)S(1)} %bitcast.19), channel_id=1, replica_groups=mesh['zh'=2,'y'=4,'c'=2,'x'=4,'zl'=8] {'y','c'}, dimensions={0} | all-to-all | bytes 1048576 | tf_op jit(solution)/shard_map/all_to_all | solution.py:56
  200.8 0.1 pad_maximum_fusion
  200.9 1.5 copy.11
Async XLA Ops:
  0.0 1.6 copy-start
  4.1 92.4 %copy-start.1 = (f32[512]{0:T(512)S(1)}, f32[512]{0:T(512)}, u32[]{:S(2)}) copy-start(f32[512]{0:T(512)} %eps.3) | copy-start | bytes 6148
  4.2 92.4 %copy-start.2 = (f32[512]{0:T(512)S(1)}, f32[512]{0:T(512)}, u32[]{:S(2)}) copy-start(f32[512]{0:T(512)} %param.7) | copy-start | bytes 6148
  19.0 29.3 %collective-permute-start = (bf16[512,512]{1,0:T(8,128)(2,1)S(1)}, bf16[512,512]{1,0:T(8,128)(2,1)S(1)}, u32[]{:S(2)}, u32[]{:S(2)}) collective-permute-start(bf16[512,512]{1,0:T(8,128)(2,1)S(1)} %bitcast.20), channel_id=1, source_target_pairs={{0,3},{1,4},{2,5},{3,6},{4,7},{5,256},{6,257},{7,258},{8,301},{9,3... | collective-permute-start | bytes 1572872 | tf_op jit(solution)/shard_map/ppermute | solution.py:52
  48.2 13.6 %collective-permute-start.1 = (bf16[512,512]{1,0:T(8,128)(2,1)S(1)}, bf16[512,512]{1,0:T(8,128)(2,1)S(1)}, u32[]{:S(2)}, u32[]{:S(2)}) collective-permute-start(bf16[512,512]{1,0:T(8,128)(2,1)S(1)} %collective-permute-done.m0), channel_id=1, source_target_pairs={{0,1},{1,2},{2,11},{3,4},{4,5},{5,6},{6,7},{7,256},{8,9},{9,10},{1... | collective-permute-start | bytes 1572872 | tf_op jit(solution)/shard_map/ppermute | solution.py:52
  61.8 15.0 %collective-permute-start.2 = (bf16[512,512]{1,0:T(8,128)(2,1)S(1)}, bf16[512,512]{1,0:T(8,128)(2,1)S(1)}, u32[]{:S(2)}, u32[]{:S(2)}) collective-permute-start(bf16[512,512]{1,0:T(8,128)(2,1)S(1)} %collective-permute-done.1.m1), channel_id=1, source_target_pairs={{0,1},{1,2},{2,11},{3,4},{4,5},{5,6},{6,7},{7,256},{8,9},{9,10},{1... | collective-permute-start | bytes 1572872 | tf_op jit(solution)/shard_map/ppermute | solution.py:52
  63.7 21.3 %collective-permute-start.7 = (bf16[512,512]{1,0:T(8,128)(2,1)S(1)}, bf16[512,512]{1,0:T(8,128)(2,1)S(1)}, u32[]{:S(2)}, u32[]{:S(2)}) collective-permute-start(bf16[512,512]{1,0:T(8,128)(2,1)S(1)} %bitcast.17), channel_id=1, source_target_pairs={{0,3},{1,4},{2,5},{3,6},{4,7},{5,256},{6,257},{7,258},{8,301},{9,3... | collective-permute-start | bytes 1572872 | tf_op jit(solution)/shard_map/ppermute | solution.py:52
  67.2 17.9 %collective-permute-start.3 = (bf16[512,512]{1,0:T(8,128)(2,1)S(1)}, bf16[512,512]{1,0:T(8,128)(2,1)S(1)}, u32[]{:S(2)}, u32[]{:S(2)}) collective-permute-start(bf16[512,512]{1,0:T(8,128)(2,1)S(1)} %collective-permute-done.m0), channel_id=1, source_target_pairs={{0,32},{1,33},{2,34},{3,35},{4,36},{5,37},{6,38},{7,39},{8,40},{9,... | collective-permute-start | bytes 1572872 | tf_op jit(solution)/shard_map/ppermute | solution.py:52
  69.1 27.4 %collective-permute-start.4 = (bf16[512,512]{1,0:T(8,128)(2,1)S(1)}, bf16[512,512]{1,0:T(8,128)(2,1)S(1)}, u32[]{:S(2)}, u32[]{:S(2)}) collective-permute-start(bf16[512,512]{1,0:T(8,128)(2,1)S(1)} %collective-permute-done.1.m1), channel_id=1, source_target_pairs={{0,32},{1,33},{2,34},{3,35},{4,36},{5,37},{6,38},{7,39},{8,40},{9,... | collective-permute-start | bytes 1572872 | tf_op jit(solution)/shard_map/ppermute | solution.py:52
  76.8 19.7 %collective-permute-start.5 = (bf16[512,512]{1,0:T(8,128)(2,1)S(1)}, bf16[512,512]{1,0:T(8,128)(2,1)S(1)}, u32[]{:S(2)}, u32[]{:S(2)}) collective-permute-start(bf16[512,512]{1,0:T(8,128)(2,1)S(1)} %collective-permute-done.2.m2), channel_id=1, source_target_pairs={{0,32},{1,33},{2,34},{3,35},{4,36},{5,37},{6,38},{7,39},{8,40},{9,... | collective-permute-start | bytes 1572872 | tf_op jit(solution)/shard_map/ppermute | solution.py:52
  85.1 16.2 %collective-permute-start.9 = (bf16[512,512]{1,0:T(8,128)(2,1)S(1)}, bf16[512,512]{1,0:T(8,128)(2,1)S(1)}, u32[]{:S(2)}, u32[]{:S(2)}) collective-permute-start(bf16[512,512]{1,0:T(8,128)(2,1)S(1)} %collective-permute-done.7.m0), channel_id=1, source_target_pairs={{0,32},{1,33},{2,34},{3,35},{4,36},{5,37},{6,38},{7,39},{8,40},{9,... | collective-permute-start | bytes 1572872 | tf_op jit(solution)/shard_map/ppermute | solution.py:52
  87.0 16.2 %collective-permute-start.8 = (bf16[512,512]{1,0:T(8,128)(2,1)S(1)}, bf16[512,512]{1,0:T(8,128)(2,1)S(1)}, u32[]{:S(2)}, u32[]{:S(2)}) collective-permute-start(bf16[512,512]{1,0:T(8,128)(2,1)S(1)} %collective-permute-done.7.m0), channel_id=1, source_target_pairs={{0,1},{1,2},{2,11},{3,4},{4,5},{5,6},{6,7},{7,256},{8,9},{9,10},{1... | collective-permute-start | bytes 1572872 | tf_op jit(solution)/shard_map/ppermute | solution.py:52
  103.2 6.3 %collective-permute-start.11 = (bf16[512,512]{1,0:T(8,128)(2,1)S(1)}, bf16[512,512]{1,0:T(8,128)(2,1)S(1)}, u32[]{:S(2)}, u32[]{:S(2)}) collective-permute-start(bf16[512,512]{1,0:T(8,128)(2,1)S(1)} %collective-permute-done.8.m1), channel_id=1, source_target_pairs={{0,32},{1,33},{2,34},{3,35},{4,36},{5,37},{6,38},{7,39},{8,40},{9,... | collective-permute-start | bytes 1572872 | tf_op jit(solution)/shard_map/ppermute | solution.py:52
  105.2 13.8 %collective-permute-start.10 = (bf16[512,512]{1,0:T(8,128)(2,1)S(1)}, bf16[512,512]{1,0:T(8,128)(2,1)S(1)}, u32[]{:S(2)}, u32[]{:S(2)}) collective-permute-start(bf16[512,512]{1,0:T(8,128)(2,1)S(1)} %collective-permute-done.8.m1), channel_id=1, source_target_pairs={{0,1},{1,2},{2,11},{3,4},{4,5},{5,6},{6,7},{7,256},{8,9},{9,10},{1... | collective-permute-start | bytes 1572872 | tf_op jit(solution)/shard_map/ppermute | solution.py:52
  119.0 6.5 %collective-permute-start.12 = (bf16[512,512]{1,0:T(8,128)(2,1)S(1)}, bf16[512,512]{1,0:T(8,128)(2,1)S(1)}, u32[]{:S(2)}, u32[]{:S(2)}) collective-permute-start(bf16[512,512]{1,0:T(8,128)(2,1)S(1)} %collective-permute-done.10.m2), channel_id=1, source_target_pairs={{0,32},{1,33},{2,34},{3,35},{4,36},{5,37},{6,38},{7,39},{8,40},{9,... | collective-permute-start | bytes 1572872 | tf_op jit(solution)/shard_map/ppermute | solution.py:52
  120.9 33.2 %collective-permute-start.6 = (bf16[512,512]{1,0:T(8,128)(2,1)S(1)}, bf16[512,512]{1,0:T(8,128)(2,1)S(1)}, u32[]{:S(2)}, u32[]{:S(2)}) collective-permute-start(bf16[512,512]{1,0:T(8,128)(2,1)S(1)} %pair_stage.2), channel_id=1, source_target_pairs={{0,293},{1,294},{2,295},{3,0},{4,1},{5,2},{6,3},{7,4},{8,269},{9,2... | collective-permute-start | bytes 1572872 | tf_op jit(solution)/shard_map/ppermute | solution.py:52
  130.2 57.9 %collective-permute-start.13 = (bf16[512,512]{1,0:T(8,128)(2,1)S(1)}, bf16[512,512]{1,0:T(8,128)(2,1)S(1)}, u32[]{:S(2)}, u32[]{:S(2)}) collective-permute-start(bf16[512,512]{1,0:T(8,128)(2,1)S(1)} %pair_stage.3), channel_id=1, source_target_pairs={{0,293},{1,294},{2,295},{3,0},{4,1},{5,2},{6,3},{7,4},{8,269},{9,2... | collective-permute-start | bytes 1572872 | tf_op jit(solution)/shard_map/ppermute | solution.py:52

commit v2 on v0

--- a/solution.py
+++ b/solution.py
@@ -121,17 +121,44 @@
     )(eps_occ, across_vir, *mine, *got)
 
 
+def transform_kernel(ints, orbitals, out):
+    rows, half, nao = ints.shape
+    full = jnp.dot(
+        ints[...].reshape(rows * half, nao), orbitals[...], preferred_element_type=jnp.float32
+    )
+    out[...] = jnp.transpose(full.reshape(rows, half, -1), (1, 0, 2)).astype(jnp.bfloat16)
+
+
+def transform(wave, half_ints, orbitals):
+    naux, group, nao = half_ints.shape
+    nvir = orbitals.shape[1]
+    half = group // 2
+    return pl.pallas_call(
+        transform_kernel,
+        grid=(1,),
+        out_shape=jax.ShapeDtypeStruct((half, naux, nvir), jnp.bfloat16),
+        in_specs=[
+            pl.BlockSpec((naux, half, nao), lambda i: (0, wave, 0)),
+            pl.BlockSpec((nao, nvir), lambda i: (0, 0)),
+        ],
+        out_specs=pl.BlockSpec((half, naux, nvir), lambda i: (0, 0, 0)),
+        cost_estimate=pl.CostEstimate(
+            flops=2 * half * naux * nao * nvir,
+            bytes_accessed=2 * (half * naux * (nao + nvir) + nao * nvir),
+            transcendentals=0,
+        ),
+        name="transform",
+    )(half_ints, orbitals)
+
+
 def body(half_ints, orbitals, eps_occ, eps_vir):
     naux, _, _ = half_ints.shape
     nvir = orbitals.shape[1]
-    local = lax.dot_general(
-        half_ints, orbitals, (((2,), (0,)), ((), ())), preferred_element_type=jnp.float32
-    ).astype(jnp.bfloat16)
-    local = jnp.transpose(local, (1, 0, 2))
     across_vir = eps_vir.reshape(1, nvir)
 
     mine, got = ([], []), ([], [])
-    pieces = [exchange(local[wave * 8 : wave * 8 + 8]).reshape(8 * naux, nvir) for wave in range(2)]
+    local = [transform(wave, half_ints, orbitals) for wave in range(2)]
+    pieces = [exchange(value).reshape(8 * naux, nvir) for value in local]
     for wave in range(2):
         mine[wave].append(send(pieces[wave], outward, wave))
     mine[0][0] = after(mine[0][0], pieces[1])

time: 194 us -> 191 us (0.985)
  waiting for transfers between devices: 60.4 us -> 52.3 us
  Pallas kernels: 9.46 us -> 15.7 us
  blocking collectives: 52.9 us -> 55.4 us
  matrix products: 2.46 us -> 0 us
  local copies, waits for them, and re-layouts: 3.54 us -> 1.56 us
    ppermute x14, waiting for transfers between devices: 60.4 us -> 52.3 us  [send(): return lax.ppermute(value, AXES, pairs_of(move, NEAR[wave]))]
    pallas_call x0 -> x2, Pallas kernels: none -> 6.22 us  [transform(): pl.pallas_call(transform_kernel, grid=(1,), out_shape=jax.ShapeDtypeStruc...]
    all_to_all x4, blocking collectives: 52.9 us -> 55.4 us  [exchange(): lax.all_to_all(value, ('y', 'c'), split_axis=0, concat_axis=0, tiled=True)]
    dot_general x1 -> x0, matrix products: 2.46 us -> none  [body(): lax.dot_general(half_ints, orbitals, (((2,), (0,)), ((), ())), preferred_...]
  transfers between devices with their start and end apart: 14 -> 14, of which waited for: 6 -> 6; matrix products, arithmetic and copies ran while one was open for 0% -> 0% of each run, Pallas kernels for 5% -> 7%
where the time goes in v2:
time: 191 us; the launch traced here: 190 us
  starting transfers between devices  64.5 us (34%)
  blocking collectives  55.4 us (29%)
  waiting for transfers between devices  52.3 us (27%)
  Pallas kernels  15.7 us (8%)
    ppermute x14, starting transfers between devices, send(): return lax.ppermute(value, AXES, pairs_of(move, NEAR[wave]))  64.5 us
    all_to_all x4, blocking collectives, exchange(): lax.all_to_all(value, ('y', 'c'), split_axis=0, concat_axis=0, tiled=True)  55.4 us
    ppermute x14, waiting for transfers between devices, send(): return lax.ppermute(value, AXES, pairs_of(move, NEAR[wave]))  52.3 us
    pallas_call x2, Pallas kernels, density(): pl.pallas_call(functools.partial(pair_kernel, wave), out_shape=jax.ShapeD...  9.46 us
    pallas_call x2, Pallas kernels, transform(): pl.pallas_call(transform_kernel, grid=(1,), out_shape=jax.ShapeDtypeStruc...  6.22 us
  transfers between devices with their start and end apart: 14, of which 6 were waited for; matrix products, arithmetic and copies ran while one was open for 0% of the time, Pallas kernels for 7%

profile of v2, /device:TPU:2, one launch (start us, length us, event | category | flops | bytes accessed | tf_op | source)
XLA Modules:
  0.0 189.8 jit_solution(9655353843214254477)
XLA Ops:
  0.0 3.1 %transform.2 = bf16[8,64,512]{2,1,0:T(8,128)(2,1)} custom-call(bf16[64,16,1024]{2,1,0:T(8,128)(2,1)} %ints.3, bf16[1024,512]{1,0:T(8,128)(2,1)} %orbitals.3), custom_call_target="tpu_custom_call" | custom-call | flops 536870912 | bytes 2621440 | tf_op jit(solution)/shard_map/transform/pallas_call | solution.py:136
  3.1 14.8 %all_to_all.20 = bf16[8,64,512]{2,1,0:T(8,128)(2,1)S(1)} all-to-all(bf16[8,64,512]{2,1,0:T(8,128)(2,1)} %transform.2), channel_id=1, replica_groups=mesh['zh'=2,'y'=4,'c'=2,'x'=4,'zl'=8] {'y','c'}, dimensions={0} | all-to-all | bytes 1048576 | tf_op jit(solution)/shard_map/all_to_all | solution.py:56
  17.9 0.0 copy-start
  17.9 0.0 copy-start.1
  17.9 11.5 %collective-permute-start = (bf16[512,512]{1,0:T(8,128)(2,1)S(1)}, bf16[512,512]{1,0:T(8,128)(2,1)S(1)}, u32[]{:S(2)}, u32[]{:S(2)}) collective-permute-start(bf16[512,512]{1,0:T(8,128)(2,1)S(1)} %bitcast.14), channel_id=1, source_target_pairs={{0,3},{1,4},{2,5},{3,6},{4,7},{5,256},{6,257},{7,258},{8,301},{9,3... | collective-permute-start | bytes 1572872 | tf_op jit(solution)/shard_map/ppermute | solution.py:52
  29.4 3.1 %transform.3 = bf16[8,64,512]{2,1,0:T(8,128)(2,1)} custom-call(bf16[64,16,1024]{2,1,0:T(8,128)(2,1)} %ints.3, bf16[1024,512]{1,0:T(8,128)(2,1)} %orbitals.3), custom_call_target="tpu_custom_call" | custom-call | flops 536870912 | bytes 2621440 | tf_op jit(solution)/shard_map/transform/pallas_call | solution.py:136
  32.5 13.8 %all_to_all.21 = bf16[8,64,512]{2,1,0:T(8,128)(2,1)S(1)} all-to-all(bf16[8,64,512]{2,1,0:T(8,128)(2,1)} %transform.3), channel_id=1, replica_groups=mesh['zh'=2,'y'=4,'c'=2,'x'=4,'zl'=8] {'y','c'}, dimensions={0} | all-to-all | bytes 1048576 | tf_op jit(solution)/shard_map/all_to_all | solution.py:56
  46.3 1.0 collective-permute-done.m0
  47.3 3.7 %collective-permute-start.1 = (bf16[512,512]{1,0:T(8,128)(2,1)S(1)}, bf16[512,512]{1,0:T(8,128)(2,1)S(1)}, u32[]{:S(2)}, u32[]{:S(2)}) collective-permute-start(bf16[512,512]{1,0:T(8,128)(2,1)S(1)} %collective-permute-done.m0), channel_id=1, source_target_pairs={{0,1},{1,2},{2,11},{3,4},{4,5},{5,6},{6,7},{7,256},{8,9},{9,10},{1... | collective-permute-start | bytes 1572872 | tf_op jit(solution)/shard_map/ppermute | solution.py:52
  51.0 5.1 %collective-permute-start.7 = (bf16[512,512]{1,0:T(8,128)(2,1)S(1)}, bf16[512,512]{1,0:T(8,128)(2,1)S(1)}, u32[]{:S(2)}, u32[]{:S(2)}) collective-permute-start(bf16[512,512]{1,0:T(8,128)(2,1)S(1)} %bitcast.11), channel_id=1, source_target_pairs={{0,3},{1,4},{2,5},{3,6},{4,7},{5,256},{6,257},{7,258},{8,301},{9,3... | collective-permute-start | bytes 1572872 | tf_op jit(solution)/shard_map/ppermute | solution.py:52
  56.1 1.9 %collective-permute-start.3 = (bf16[512,512]{1,0:T(8,128)(2,1)S(1)}, bf16[512,512]{1,0:T(8,128)(2,1)S(1)}, u32[]{:S(2)}, u32[]{:S(2)}) collective-permute-start(bf16[512,512]{1,0:T(8,128)(2,1)S(1)} %collective-permute-done.m0), channel_id=1, source_target_pairs={{0,32},{1,33},{2,34},{3,35},{4,36},{5,37},{6,38},{7,39},{8,40},{9,... | collective-permute-start | bytes 1572872 | tf_op jit(solution)/shard_map/ppermute | solution.py:52
  58.0 7.3 %collective-permute-done.1.m1 = bf16[512,512]{1,0:T(8,128)(2,1)S(1)} collective-permute-done((bf16[512,512]{1,0:T(8,128)(2,1)S(1)}, bf16[512,512]{1,0:T(8,128)(2,1)S(1)}, u32[]{:S(2)}, u32[]{:S(2)}) %collective-permute-start.1) | collective-permute-done | bytes 524320 | tf_op jit(solution)/shard_map/ppermute | solution.py:52
  65.3 11.8 %collective-permute-start.2 = (bf16[512,512]{1,0:T(8,128)(2,1)S(1)}, bf16[512,512]{1,0:T(8,128)(2,1)S(1)}, u32[]{:S(2)}, u32[]{:S(2)}) collective-permute-start(bf16[512,512]{1,0:T(8,128)(2,1)S(1)} %collective-permute-done.1.m1), channel_id=1, source_target_pairs={{0,1},{1,2},{2,11},{3,4},{4,5},{5,6},{6,7},{7,256},{8,9},{9,10},{1... | collective-permute-start | bytes 1572872 | tf_op jit(solution)/shard_map/ppermute | solution.py:52
  77.1 0.0 collective-permute-done.7.m0
  77.2 0.0 collective-permute-done.3.g0
  77.2 1.9 %collective-permute-start.4 = (bf16[512,512]{1,0:T(8,128)(2,1)S(1)}, bf16[512,512]{1,0:T(8,128)(2,1)S(1)}, u32[]{:S(2)}, u32[]{:S(2)}) collective-permute-start(bf16[512,512]{1,0:T(8,128)(2,1)S(1)} %collective-permute-done.1.m1), channel_id=1, source_target_pairs={{0,32},{1,33},{2,34},{3,35},{4,36},{5,37},{6,38},{7,39},{8,40},{9,... | collective-permute-start | bytes 1572872 | tf_op jit(solution)/shard_map/ppermute | solution.py:52
  79.1 2.4 %collective-permute-start.9 = (bf16[512,512]{1,0:T(8,128)(2,1)S(1)}, bf16[512,512]{1,0:T(8,128)(2,1)S(1)}, u32[]{:S(2)}, u32[]{:S(2)}) collective-permute-start(bf16[512,512]{1,0:T(8,128)(2,1)S(1)} %collective-permute-done.7.m0), channel_id=1, source_target_pairs={{0,32},{1,33},{2,34},{3,35},{4,36},{5,37},{6,38},{7,39},{8,40},{9,... | collective-permute-start | bytes 1572872 | tf_op jit(solution)/shard_map/ppermute | solution.py:52
  81.5 5.5 %collective-permute-start.8 = (bf16[512,512]{1,0:T(8,128)(2,1)S(1)}, bf16[512,512]{1,0:T(8,128)(2,1)S(1)}, u32[]{:S(2)}, u32[]{:S(2)}) collective-permute-start(bf16[512,512]{1,0:T(8,128)(2,1)S(1)} %collective-permute-done.7.m0), channel_id=1, source_target_pairs={{0,1},{1,2},{2,11},{3,4},{4,5},{5,6},{6,7},{7,256},{8,9},{9,10},{1... | collective-permute-start | bytes 1572872 | tf_op jit(solution)/shard_map/ppermute | solution.py:52
  87.1 0.0 collective-permute-done.2.m2
  87.1 1.9 %collective-permute-start.5 = (bf16[512,512]{1,0:T(8,128)(2,1)S(1)}, bf16[512,512]{1,0:T(8,128)(2,1)S(1)}, u32[]{:S(2)}, u32[]{:S(2)}) collective-permute-start(bf16[512,512]{1,0:T(8,128)(2,1)S(1)} %collective-permute-done.2.m2), channel_id=1, source_target_pairs={{0,32},{1,33},{2,34},{3,35},{4,36},{5,37},{6,38},{7,39},{8,40},{9,... | collective-permute-start | bytes 1572872 | tf_op jit(solution)/shard_map/ppermute | solution.py:52
  89.0 0.0 collective-permute-done.4.g1
  89.0 0.0 collective-permute-done.9.g0
  89.0 4.8 %collective-permute-done.8.m1 = bf16[512,512]{1,0:T(8,128)(2,1)S(1)} collective-permute-done((bf16[512,512]{1,0:T(8,128)(2,1)S(1)}, bf16[512,512]{1,0:T(8,128)(2,1)S(1)}, u32[]{:S(2)}, u32[]{:S(2)}) %collective-permute-start.8) | collective-permute-done | bytes 524320 | tf_op jit(solution)/shard_map/ppermute | solution.py:52
  93.8 4.3 %collective-permute-start.10 = (bf16[512,512]{1,0:T(8,128)(2,1)S(1)}, bf16[512,512]{1,0:T(8,128)(2,1)S(1)}, u32[]{:S(2)}, u32[]{:S(2)}) collective-permute-start(bf16[512,512]{1,0:T(8,128)(2,1)S(1)} %collective-permute-done.8.m1), channel_id=1, source_target_pairs={{0,1},{1,2},{2,11},{3,4},{4,5},{5,6},{6,7},{7,256},{8,9},{9,10},{1... | collective-permute-start | bytes 1572872 | tf_op jit(solution)/shard_map/ppermute | solution.py:52
  98.1 0.0 collective-permute-done.5.g2
  98.1 0.0 copy-done
  98.1 0.0 copy-done.1
  98.1 4.7 %pair_stage.2 = bf16[512,512]{1,0:T(8,128)(2,1)S(1)} custom-call(f32[512]{0:T(512)S(1)} %copy-done, f32[1,512]{1,0:T(1,128)S(1)} %bitcast.7, bf16[512,512]{1,0:T(8,128)(2,1)S(1)} %collective-permute-done.m0, bf16[512,512]{1,0:T(8,128)(2,1)S(1)} %collective-permute-done.1.m1, bf16[512,512]{1,0:T(8,128)(2,1)S(1)} %collective-permute-done.2.m2, ...), custom_call_target="tpu_custom_call" | custom-call | flops 3489660928 | bytes 3670016 | tf_op jit(solution)/shard_map/pair_stage/pallas_call | solution.py:110
  102.9 1.9 %collective-permute-start.11 = (bf16[512,512]{1,0:T(8,128)(2,1)S(1)}, bf16[512,512]{1,0:T(8,128)(2,1)S(1)}, u32[]{:S(2)}, u32[]{:S(2)}) collective-permute-start(bf16[512,512]{1,0:T(8,128)(2,1)S(1)} %collective-permute-done.8.m1), channel_id=1, source_target_pairs={{0,32},{1,33},{2,34},{3,35},{4,36},{5,37},{6,38},{7,39},{8,40},{9,... | collective-permute-start | bytes 1572872 | tf_op jit(solution)/shard_map/ppermute | solution.py:52
  104.8 1.4 collective-permute-done.10.m2
  106.2 1.9 %collective-permute-start.12 = (bf16[512,512]{1,0:T(8,128)(2,1)S(1)}, bf16[512,512]{1,0:T(8,128)(2,1)S(1)}, u32[]{:S(2)}, u32[]{:S(2)}) collective-permute-start(bf16[512,512]{1,0:T(8,128)(2,1)S(1)} %collective-permute-done.10.m2), channel_id=1, source_target_pairs={{0,32},{1,33},{2,34},{3,35},{4,36},{5,37},{6,38},{7,39},{8,40},{9,... | collective-permute-start | bytes 1572872 | tf_op jit(solution)/shard_map/ppermute | solution.py:52
  108.1 6.5 %collective-permute-start.6 = (bf16[512,512]{1,0:T(8,128)(2,1)S(1)}, bf16[512,512]{1,0:T(8,128)(2,1)S(1)}, u32[]{:S(2)}, u32[]{:S(2)}) collective-permute-start(bf16[512,512]{1,0:T(8,128)(2,1)S(1)} %pair_stage.2), channel_id=1, source_target_pairs={{0,293},{1,294},{2,295},{3,0},{4,1},{5,2},{6,3},{7,4},{8,269},{9,2... | collective-permute-start | bytes 1572872 | tf_op jit(solution)/shard_map/ppermute | solution.py:52
  114.6 0.0 collective-permute-done.11.g1
  114.6 0.0 collective-permute-done.12.g2
  114.6 4.7 %pair_stage.3 = bf16[512,512]{1,0:T(8,128)(2,1)S(1)} custom-call(f32[512]{0:T(512)S(1)} %copy-done, f32[1,512]{1,0:T(1,128)S(1)} %bitcast.8, bf16[512,512]{1,0:T(8,128)(2,1)S(1)} %collective-permute-done.7.m0, bf16[512,512]{1,0:T(8,128)(2,1)S(1)} %collective-permute-done.8.m1, bf16[512,512]{1,0:T(8,128)(2,1)S(1)} %collective-permute-done.10.m2, ...), custom_call_target="tpu_custom_call" | custom-call | flops 3489660928 | bytes 3670016 | tf_op jit(solution)/shard_map/pair_stage/pallas_call | solution.py:110
  119.3 4.2 %collective-permute-start.13 = (bf16[512,512]{1,0:T(8,128)(2,1)S(1)}, bf16[512,512]{1,0:T(8,128)(2,1)S(1)}, u32[]{:S(2)}, u32[]{:S(2)}) collective-permute-start(bf16[512,512]{1,0:T(8,128)(2,1)S(1)} %pair_stage.3), channel_id=1, source_target_pairs={{0,293},{1,294},{2,295},{3,0},{4,1},{5,2},{6,3},{7,4},{8,269},{9,2... | collective-permute-start | bytes 1572872 | tf_op jit(solution)/shard_map/ppermute | solution.py:52
  123.5 28.0 %collective-permute-done.6 = bf16[512,512]{1,0:T(8,128)(2,1)S(1)} collective-permute-done((bf16[512,512]{1,0:T(8,128)(2,1)S(1)}, bf16[512,512]{1,0:T(8,128)(2,1)S(1)}, u32[]{:S(2)}, u32[]{:S(2)}) %collective-permute-start.6) | collective-permute-done | bytes 524320 | tf_op jit(solution)/shard_map/ppermute | solution.py:52
  151.5 14.1 %all_to_all.22 = bf16[8,64,512]{2,1,0:T(8,128)(2,1)S(1)} all-to-all(bf16[8,64,512]{2,1,0:T(8,128)(2,1)S(1)} %bitcast.12), channel_id=1, replica_groups=mesh['zh'=2,'y'=4,'c'=2,'x'=4,'zl'=8] {'y','c'}, dimensions={0} | all-to-all | bytes 1048576 | tf_op jit(solution)/shard_map/all_to_all | solution.py:56
  165.6 9.8 %collective-permute-done.13 = bf16[512,512]{1,0:T(8,128)(2,1)S(1)} collective-permute-done((bf16[512,512]{1,0:T(8,128)(2,1)S(1)}, bf16[512,512]{1,0:T(8,128)(2,1)S(1)}, u32[]{:S(2)}, u32[]{:S(2)}) %collective-permute-start.13) | collective-permute-done | bytes 524320 | tf_op jit(solution)/shard_map/ppermute | solution.py:52
  175.4 12.8 %all_to_all.23 = bf16[8,64,512]{2,1,0:T(8,128)(2,1)S(1)} all-to-all(bf16[8,64,512]{2,1,0:T(8,128)(2,1)S(1)} %bitcast.13), channel_id=1, replica_groups=mesh['zh'=2,'y'=4,'c'=2,'x'=4,'zl'=8] {'y','c'}, dimensions={0} | all-to-all | bytes 1048576 | tf_op jit(solution)/shard_map/all_to_all | solution.py:56
  188.1 0.1 pad_maximum_fusion
  188.2 1.5 copy.7
Async XLA Ops:
  17.9 80.2 %copy-start = (f32[512]{0:T(512)S(1)}, f32[512]{0:T(512)}, u32[]{:S(2)}) copy-start(f32[512]{0:T(512)} %eps.3) | copy-start | bytes 6148
  17.9 80.2 %copy-start.1 = (f32[512]{0:T(512)S(1)}, f32[512]{0:T(512)}, u32[]{:S(2)}) copy-start(f32[512]{0:T(512)} %param.7) | copy-start | bytes 6148
  17.9 29.4 %collective-permute-start = (bf16[512,512]{1,0:T(8,128)(2,1)S(1)}, bf16[512,512]{1,0:T(8,128)(2,1)S(1)}, u32[]{:S(2)}, u32[]{:S(2)}) collective-permute-start(bf16[512,512]{1,0:T(8,128)(2,1)S(1)} %bitcast.14), channel_id=1, source_target_pairs={{0,3},{1,4},{2,5},{3,6},{4,7},{5,256},{6,257},{7,258},{8,301},{9,3... | collective-permute-start | bytes 1572872 | tf_op jit(solution)/shard_map/ppermute | solution.py:52
  47.3 18.0 %collective-permute-start.1 = (bf16[512,512]{1,0:T(8,128)(2,1)S(1)}, bf16[512,512]{1,0:T(8,128)(2,1)S(1)}, u32[]{:S(2)}, u32[]{:S(2)}) collective-permute-start(bf16[512,512]{1,0:T(8,128)(2,1)S(1)} %collective-permute-done.m0), channel_id=1, source_target_pairs={{0,1},{1,2},{2,11},{3,4},{4,5},{5,6},{6,7},{7,256},{8,9},{9,10},{1... | collective-permute-start | bytes 1572872 | tf_op jit(solution)/shard_map/ppermute | solution.py:52
  51.0 26.1 %collective-permute-start.7 = (bf16[512,512]{1,0:T(8,128)(2,1)S(1)}, bf16[512,512]{1,0:T(8,128)(2,1)S(1)}, u32[]{:S(2)}, u32[]{:S(2)}) collective-permute-start(bf16[512,512]{1,0:T(8,128)(2,1)S(1)} %bitcast.11), channel_id=1, source_target_pairs={{0,3},{1,4},{2,5},{3,6},{4,7},{5,256},{6,257},{7,258},{8,301},{9,3... | collective-permute-start | bytes 1572872 | tf_op jit(solution)/shard_map/ppermute | solution.py:52
  56.1 21.1 %collective-permute-start.3 = (bf16[512,512]{1,0:T(8,128)(2,1)S(1)}, bf16[512,512]{1,0:T(8,128)(2,1)S(1)}, u32[]{:S(2)}, u32[]{:S(2)}) collective-permute-start(bf16[512,512]{1,0:T(8,128)(2,1)S(1)} %collective-permute-done.m0), channel_id=1, source_target_pairs={{0,32},{1,33},{2,34},{3,35},{4,36},{5,37},{6,38},{7,39},{8,40},{9,... | collective-permute-start | bytes 1572872 | tf_op jit(solution)/shard_map/ppermute | solution.py:52
  65.3 21.7 %collective-permute-start.2 = (bf16[512,512]{1,0:T(8,128)(2,1)S(1)}, bf16[512,512]{1,0:T(8,128)(2,1)S(1)}, u32[]{:S(2)}, u32[]{:S(2)}) collective-permute-start(bf16[512,512]{1,0:T(8,128)(2,1)S(1)} %collective-permute-done.1.m1), channel_id=1, source_target_pairs={{0,1},{1,2},{2,11},{3,4},{4,5},{5,6},{6,7},{7,256},{8,9},{9,10},{1... | collective-permute-start | bytes 1572872 | tf_op jit(solution)/shard_map/ppermute | solution.py:52
  77.2 11.8 %collective-permute-start.4 = (bf16[512,512]{1,0:T(8,128)(2,1)S(1)}, bf16[512,512]{1,0:T(8,128)(2,1)S(1)}, u32[]{:S(2)}, u32[]{:S(2)}) collective-permute-start(bf16[512,512]{1,0:T(8,128)(2,1)S(1)} %collective-permute-done.1.m1), channel_id=1, source_target_pairs={{0,32},{1,33},{2,34},{3,35},{4,36},{5,37},{6,38},{7,39},{8,40},{9,... | collective-permute-start | bytes 1572872 | tf_op jit(solution)/shard_map/ppermute | solution.py:52
  79.1 9.9 %collective-permute-start.9 = (bf16[512,512]{1,0:T(8,128)(2,1)S(1)}, bf16[512,512]{1,0:T(8,128)(2,1)S(1)}, u32[]{:S(2)}, u32[]{:S(2)}) collective-permute-start(bf16[512,512]{1,0:T(8,128)(2,1)S(1)} %collective-permute-done.7.m0), channel_id=1, source_target_pairs={{0,32},{1,33},{2,34},{3,35},{4,36},{5,37},{6,38},{7,39},{8,40},{9,... | collective-permute-start | bytes 1572872 | tf_op jit(solution)/shard_map/ppermute | solution.py:52
  81.5 12.3 %collective-permute-start.8 = (bf16[512,512]{1,0:T(8,128)(2,1)S(1)}, bf16[512,512]{1,0:T(8,128)(2,1)S(1)}, u32[]{:S(2)}, u32[]{:S(2)}) collective-permute-start(bf16[512,512]{1,0:T(8,128)(2,1)S(1)} %collective-permute-done.7.m0), channel_id=1, source_target_pairs={{0,1},{1,2},{2,11},{3,4},{4,5},{5,6},{6,7},{7,256},{8,9},{9,10},{1... | collective-permute-start | bytes 1572872 | tf_op jit(solution)/shard_map/ppermute | solution.py:52
  87.1 11.1 %collective-permute-start.5 = (bf16[512,512]{1,0:T(8,128)(2,1)S(1)}, bf16[512,512]{1,0:T(8,128)(2,1)S(1)}, u32[]{:S(2)}, u32[]{:S(2)}) collective-permute-start(bf16[512,512]{1,0:T(8,128)(2,1)S(1)} %collective-permute-done.2.m2), channel_id=1, source_target_pairs={{0,32},{1,33},{2,34},{3,35},{4,36},{5,37},{6,38},{7,39},{8,40},{9,... | collective-permute-start | bytes 1572872 | tf_op jit(solution)/shard_map/ppermute | solution.py:52
  93.8 12.4 %collective-permute-start.10 = (bf16[512,512]{1,0:T(8,128)(2,1)S(1)}, bf16[512,512]{1,0:T(8,128)(2,1)S(1)}, u32[]{:S(2)}, u32[]{:S(2)}) collective-permute-start(bf16[512,512]{1,0:T(8,128)(2,1)S(1)} %collective-permute-done.8.m1), channel_id=1, source_target_pairs={{0,1},{1,2},{2,11},{3,4},{4,5},{5,6},{6,7},{7,256},{8,9},{9,10},{1... | collective-permute-start | bytes 1572872 | tf_op jit(solution)/shard_map/ppermute | solution.py:52
  102.9 11.7 %collective-permute-start.11 = (bf16[512,512]{1,0:T(8,128)(2,1)S(1)}, bf16[512,512]{1,0:T(8,128)(2,1)S(1)}, u32[]{:S(2)}, u32[]{:S(2)}) collective-permute-start(bf16[512,512]{1,0:T(8,128)(2,1)S(1)} %collective-permute-done.8.m1), channel_id=1, source_target_pairs={{0,32},{1,33},{2,34},{3,35},{4,36},{5,37},{6,38},{7,39},{8,40},{9,... | collective-permute-start | bytes 1572872 | tf_op jit(solution)/shard_map/ppermute | solution.py:52
  106.2 8.4 %collective-permute-start.12 = (bf16[512,512]{1,0:T(8,128)(2,1)S(1)}, bf16[512,512]{1,0:T(8,128)(2,1)S(1)}, u32[]{:S(2)}, u32[]{:S(2)}) collective-permute-start(bf16[512,512]{1,0:T(8,128)(2,1)S(1)} %collective-permute-done.10.m2), channel_id=1, source_target_pairs={{0,32},{1,33},{2,34},{3,35},{4,36},{5,37},{6,38},{7,39},{8,40},{9,... | collective-permute-start | bytes 1572872 | tf_op jit(solution)/shard_map/ppermute | solution.py:52
  108.1 43.4 %collective-permute-start.6 = (bf16[512,512]{1,0:T(8,128)(2,1)S(1)}, bf16[512,512]{1,0:T(8,128)(2,1)S(1)}, u32[]{:S(2)}, u32[]{:S(2)}) collective-permute-start(bf16[512,512]{1,0:T(8,128)(2,1)S(1)} %pair_stage.2), channel_id=1, source_target_pairs={{0,293},{1,294},{2,295},{3,0},{4,1},{5,2},{6,3},{7,4},{8,269},{9,2... | collective-permute-start | bytes 1572872 | tf_op jit(solution)/shard_map/ppermute | solution.py:52
  119.3 56.0 %collective-permute-start.13 = (bf16[512,512]{1,0:T(8,128)(2,1)S(1)}, bf16[512,512]{1,0:T(8,128)(2,1)S(1)}, u32[]{:S(2)}, u32[]{:S(2)}) collective-permute-start(bf16[512,512]{1,0:T(8,128)(2,1)S(1)} %pair_stage.3), channel_id=1, source_target_pairs={{0,293},{1,294},{2,295},{3,0},{4,1},{5,2},{6,3},{7,4},{8,269},{9,2... | collective-permute-start | bytes 1572872 | tf_op jit(solution)/shard_map/ppermute | solution.py:52
